TPU v7x, 128 devices: a whole 4x4x4 slice. The times are simulated.
128 devices in a mesh: rep: 8 (over z, core), tensor: 16 (over y, x).
Axes of the slice: x: 4, y: 4, z: 4, core: 2. Of those that a mesh axis runs over, the one named last changes fastest.
Arguments:
- x_pre: bfloat16 [8192, 2560], P(('rep', 'tensor')), may hold values from -6 to 6
- x_dec: bfloat16 [16, 2560], replicated, may hold values from -6 to 6
- prefix_kv: bfloat16 [8, 4096, 32, 160], P('rep', None, 'tensor'), may hold values from -400 to 400
- cache_kv: bfloat16 [16, 4096, 32, 160], P(None, 'rep', 'tensor'), may hold values from -400 to 400
- dec_len: int32 [16], replicated, may hold values from 1 to 4096, as said below
- offsets: int32 [8], P('rep'), may hold values from 0 to 4096, as said below
- segments: int32 [8, 1024], P('rep'), may hold values from 0 to 3, never falling along the last dimension, each value on 1 to 512 neighbouring positions
- w_qkv: bfloat16 [2560, 7680], P(None, 'tensor'), may hold values from -0.125 to 0.125
- w_out: bfloat16 [2560, 2560], P('tensor'), may hold values from -0.125 to 0.125
- w_up: bfloat16 [2560, 10240], P(None, 'tensor'), may hold values from -0.125 to 0.125
- up_bias: float32 [10240], P('tensor'), may hold values from -3 to 3
- w_down: bfloat16 [10240, 2560], P('tensor'), may hold values from -0.0625 to 0.0625
- biases: float32 [2, 2560], replicated, may hold values from -3 to 3
- gains: float32 [2, 2560], replicated, may hold values from 0.1 to 1.9
- shifts: float32 [2, 2560], replicated, may hold values from -2.5 to 2.5
- w_next: bfloat16 [2560, 7680], P(None, 'tensor'), may hold values from -0.125 to 0.125
Outputs:
- layer_out: bfloat16 [8192, 2560], P(('rep', 'tensor'))
- next_qkv: bfloat16 [8192, 7680], P('rep', 'tensor')
- dec_out: bfloat16 [16, 2560], replicated
- dec_next_qkv: bfloat16 [16, 7680], P(None, 'tensor')
Inputs may be any that keep to these rules, and one draw needn't show every extreme that they name: Request r's cache holds live entries at positions below dec_len[r]; in every draw one request's cache is full (4096) and one request has a single live position. `offsets`: in every draw one span has a full earlier cache (4096 positions) and one span has none.
All inputs are finite; a program needn't handle non-finite values.
Results may differ from a plain program's by a relative error of at most 0.025.
Values may be sent and summed in bfloat16 or wider, within the bound.
A program may use at most 192 MiB of HBM per device.

v0:
```python
import jax
import jax.numpy as jnp
from jax import lax
from jax.sharding import PartitionSpec as P

NEG = -1e30


def combined_all(value, axis, join):
    pieces = jax.tree.map(lambda part: lax.all_gather(part, axis), value)
    head = jax.tree.map(lambda part: part[0], pieces)
    tail = jax.tree.map(lambda part: part[1:], pieces)
    total, _ = lax.scan(lambda total, slab: (join(total, slab), None), head, tail)
    return total


def layer_norm(values, gain_row, shift_row):
    average = jnp.mean(values, axis=-1, keepdims=True)
    centred = values - average
    spread = jnp.mean(centred * centred, axis=-1, keepdims=True)
    return centred * lax.rsqrt(spread + 1e-05) * gain_row + shift_row


def visible(seg_query, query_pos, seg_all, offset, prefix_len):
    prefix_pos = jnp.arange(prefix_len)
    from_prefix = (prefix_pos[None, :] < offset) & (seg_query[:, None] == 0)
    span_pos = jnp.arange(seg_all.shape[0])
    from_span = (seg_all[None, :] == seg_query[:, None]) & (span_pos[None, :] <= query_pos[:, None])
    return jnp.concatenate([from_prefix, from_span], axis=1)


def combine(earlier, later):
    high_early, total_early, output_early = earlier
    high_later, total_later, output_later = later
    highest = jnp.maximum(high_early, high_later)
    factor_early = jnp.exp(high_early - highest)
    factor_later = jnp.exp(high_later - highest)
    return (
        highest,
        total_early * factor_early + total_later * factor_later,
        output_early * factor_early[..., None] + output_later * factor_later[..., None],
    )


def block_state(queries, keys, values, valid, scale):
    scores = jnp.einsum("rhd,rphd->rhp", queries, keys, preferred_element_type=jnp.float32) * scale
    scores = jnp.where(valid[:, None, :], scores, NEG)
    highest = jnp.max(scores, axis=-1)
    weights = jnp.where(valid[:, None, :], jnp.exp(scores - highest[..., None]), 0.0)
    totals = jnp.sum(weights, axis=-1)
    output = jnp.einsum("rhp,rphd->rhd", weights, values.astype(jnp.float32))
    return (highest, totals, output)


def per_device(
    x_pre,
    x_dec,
    prefix_kv,
    cache_kv,
    dec_len,
    offsets,
    segments,
    w_qkv,
    w_out,
    w_up,
    up_bias,
    w_down,
    biases,
    gains,
    shifts,
    w_next,
):
    heads_dev = prefix_kv.shape[2]
    head_dim = prefix_kv.shape[3] // 2
    prefix_len = prefix_kv.shape[1]
    span_len = segments.shape[1]
    scale = head_dim ** (-0.5)

    def up_rows(piece):
        return jax.nn.gelu(
            jnp.dot(piece, w_up, preferred_element_type=jnp.float32) + up_bias, approximate=False
        ).astype(jnp.bfloat16)

    def next_rows(piece):
        return jnp.dot(piece, w_next, preferred_element_type=jnp.float32).astype(jnp.bfloat16)

    qkv_all = jnp.dot(
        lax.all_gather(x_pre, "tensor", axis=0, tiled=True),
        w_qkv,
        preferred_element_type=jnp.float32,
    ).astype(jnp.bfloat16)
    dec_qkv = jnp.dot(x_dec, w_qkv, preferred_element_type=jnp.float32).astype(jnp.bfloat16)
    dec_four = dec_qkv.reshape(dec_qkv.shape[0], heads_dev, 3, head_dim)
    dec_query = dec_four[:, :, 0]
    positions = cache_kv.shape[1]
    cache_base = lax.axis_index("rep") * positions
    valid = (cache_base + jnp.arange(positions))[None, :] < dec_len[:, None]
    state = block_state(dec_query, cache_kv[..., :head_dim], cache_kv[..., head_dim:], valid, scale)
    is_first = lax.axis_index("rep") == 0
    own_score = (
        jnp.sum(dec_query.astype(jnp.float32) * dec_four[:, :, 1].astype(jnp.float32), axis=-1)
        * scale
    )
    own_state = (
        jnp.where(is_first, own_score, NEG),
        jnp.where(is_first, jnp.ones_like(own_score), jnp.zeros_like(own_score)),
        jnp.where(is_first, dec_four[:, :, 2].astype(jnp.float32), 0.0),
    )
    state = combine(state, own_state)
    merged = combined_all(state, "rep", combine)
    dec_attn = (
        (merged[2] / merged[1][..., None])
        .astype(jnp.bfloat16)
        .reshape(dec_qkv.shape[0], heads_dev * head_dim)
    )
    qkv_four = qkv_all.reshape(span_len, heads_dev, 3, head_dim)
    queries = qkv_four[:, :, 0]
    prefix = prefix_kv[0]
    keys = jnp.concatenate([prefix[:, :, :head_dim], qkv_four[:, :, 1]], axis=0)
    values = jnp.concatenate([prefix[:, :, head_dim:], qkv_four[:, :, 2]], axis=0)
    seg_all = segments[0]
    offset = offsets[0]
    query_block = min(512, span_len)

    def attend_block(index):
        begin = index * query_block
        query_rows = lax.dynamic_slice_in_dim(queries, begin, query_block, 0)
        seg_query = lax.dynamic_slice_in_dim(seg_all, begin, query_block, 0)
        mask = visible(seg_query, begin + jnp.arange(query_block), seg_all, offset, prefix_len)
        scores = (
            jnp.einsum("qhd,khd->hqk", query_rows, keys, preferred_element_type=jnp.float32) * scale
        )
        scores = jnp.where(mask[None], scores, NEG)
        highest = jnp.max(scores, axis=-1, keepdims=True)
        weights = jnp.where(mask[None], jnp.exp(scores - highest), 0.0)
        weights = (weights / jnp.sum(weights, axis=-1, keepdims=True)).astype(jnp.bfloat16)
        return jnp.einsum(
            "hqk,khd->qhd", weights, values, preferred_element_type=jnp.float32
        ).astype(jnp.bfloat16)

    blocks = lax.map(attend_block, jnp.arange(span_len // query_block))
    attn = blocks.reshape(span_len, heads_dev * head_dim)
    attn_part = lax.psum_scatter(
        jnp.dot(attn, w_out, preferred_element_type=jnp.float32).astype(jnp.bfloat16),
        "tensor",
        scatter_dimension=0,
        tiled=True,
    ).astype(jnp.float32)
    dec_sum = lax.psum(
        jnp.dot(dec_attn, w_out, preferred_element_type=jnp.float32).astype(jnp.bfloat16), "tensor"
    ).astype(jnp.float32)
    h_first = layer_norm(
        x_pre.astype(jnp.float32) + attn_part + biases[0], gains[0], shifts[0]
    ).astype(jnp.bfloat16)
    hidden = up_rows(lax.all_gather(h_first, "tensor", axis=0, tiled=True))
    dec_first = layer_norm(
        x_dec.astype(jnp.float32) + dec_sum + biases[0], gains[0], shifts[0]
    ).astype(jnp.bfloat16)
    mlp_part = lax.psum_scatter(
        jnp.dot(hidden, w_down, preferred_element_type=jnp.float32).astype(jnp.bfloat16),
        "tensor",
        scatter_dimension=0,
        tiled=True,
    ).astype(jnp.float32)
    layer_out = layer_norm(
        h_first.astype(jnp.float32) + mlp_part + biases[1], gains[1], shifts[1]
    ).astype(jnp.bfloat16)
    dec_hidden = up_rows(dec_first)
    dec_mlp = lax.psum(
        jnp.dot(dec_hidden, w_down, preferred_element_type=jnp.float32).astype(jnp.bfloat16),
        "tensor",
    ).astype(jnp.float32)
    dec_out = layer_norm(
        dec_first.astype(jnp.float32) + dec_mlp + biases[1], gains[1], shifts[1]
    ).astype(jnp.bfloat16)
    next_qkv = next_rows(lax.all_gather(layer_out, "tensor", axis=0, tiled=True))
    dec_next_qkv = next_rows(dec_out)
    return (layer_out, next_qkv, dec_out, dec_next_qkv)


def solution(mesh):
    placed = (
        P(("rep", "tensor"), None),
        P(),
        P("rep", None, "tensor", None),
        P(None, "rep", "tensor", None),
        P(),
        P("rep"),
        P("rep", None),
        P(None, "tensor"),
        P("tensor", None),
        P(None, "tensor"),
        P("tensor"),
        P("tensor", None),
        P(),
        P(),
        P(),
        P(None, "tensor"),
    )
    return jax.shard_map(
        per_device,
        mesh=mesh,
        in_specs=placed,
        out_specs=(P(("rep", "tensor"), None), P("rep", "tensor"), P(), P(None, "tensor")),
        check_vma=False,
    )
```

profile of v0, /device:TPU:1, one launch (start us, length us, event | category | flops | bytes accessed | tf_op | source)
XLA Modules:
  0.0 648.3 jit_solution(16715024463593659003)
XLA Ops:
  7.2 0.7 all-gather.5.cloned.1.call-update
  8.0 3.7 fusion.182
  11.7 58.0 %all-gather.5.cloned.1.call-done = bf16[1024,2560]{1,0:T(8,128)(2,1)} async-done(((bf16[64,2560]{1,0:T(8,128)(2,1)}), bf16[1024,2560]{1,0:T(8,128)(2,1)}) %all-gather.5.cloned.1.call-update) | async-done | bytes 5242896 | tf_op jit(solution)/shard_map/all_gather | solution.py:88
  69.7 6.1 convolution_convert_fusion.5
  75.8 0.8 slice_bitcast_fusion
  77.2 2.0 pad_maximum_fusion
  79.2 101.0 %while.24 = (s32[]{:T(128)}, bf16[2,512,2,80]{1,3,2,0:T(8,128)(2,1)}, s32[]{:T(128)}, s32[2]{0:T(128)S(1)}, s32[1024]{0:T(1024)S(1)}, /*index=5*/s32[1,1024]{1,0...) while((s32[]{:T(128)}, ...), condition=%wide.region_3.4_spmd, body=%wide.region_0.3_spmd.sunk | while | flops 1731291136 | bytes 107183400 | solution.py:141
  80.4 11.4 %fusion.215 = f32[2,512,5120]{2,1,0:T(8,128)} fusion(bf16[5120,2,80]{0,2,1:T(8,128)(2,1)} %get-tuple-element.300, bf16[1024,2,80]{0,2,1:T(8,128)(2,1)} %get-tuple-element.299, s32[]{:T(128)S(6)} %select_n.124), kind=kOutput, calls=%fused_computation.16.clone.1 | convolution fusion | flops 838860800 | bytes 22773764 | tf_op jit(solution)/shard_map/while/body/eval_jaxpr/qhd,khd->hqk/dot_general | solution.py:131
  92.5 0.7 iota_compare_fusion.3
  93.2 1.3 broadcast_and_fusion.2
  94.7 25.4 %fusion.217 = (f32[2,512]{1,0:T(2,128)S(1)}, f32[2,512,5120]{2,1,0:T(8,128)}) fusion(f32[2,512,5120]{2,1,0:T(8,128)} %fusion.215, pred[512,5120]{1,0:T(8,128)(4,1)S(1)} %pad_add_fusion.2), kind=kOutput, calls=%fused_computation.273.clone.1 | output fusion | flops 36705280 | bytes 44568576 | tf_op jit(solution)/shard_map/while/body/eval_jaxpr/sub | solution.py:135
  120.1 8.8 %fusion.218 = bf16[2,512,2,80]{1,3,2,0:T(8,128)(2,1)S(1)} fusion(bf16[2,512,2,80]{1,3,2,0:T(8,128)(2,1)S(1)} %copy-done.6, s32[]{:T(128)S(6)} %copy.93, bf16[5120,2,80]{0,2,1:T(8,128)(2,1)S(1)} %copy-done.3, f32[2,512,5120]{2,1,0:T(8,128)} %get-tuple-element.254, f32[2,512]{1,0:T(2,128)S(1)} %get-tuple-element.255), kind=kOutput, calls=%fused_computation.15.clone.1 | convolution fusion | flops 849428480 | bytes 22777860 | tf_op jit(solution)/shard_map/while/body/eval_jaxpr/hqk,khd->qhd/dot_general | solution.py:137
  128.9 0.7 copy-done.7
  130.9 11.4 %fusion.215 = f32[2,512,5120]{2,1,0:T(8,128)} fusion(bf16[5120,2,80]{0,2,1:T(8,128)(2,1)} %get-tuple-element.300, bf16[1024,2,80]{0,2,1:T(8,128)(2,1)} %get-tuple-element.299, s32[]{:T(128)S(6)} %select_n.124), kind=kOutput, calls=%fused_computation.16.clone.1 | convolution fusion | flops 838860800 | bytes 22773764 | tf_op jit(solution)/shard_map/while/body/eval_jaxpr/qhd,khd->hqk/dot_general | solution.py:131
  143.0 0.7 iota_compare_fusion.3
  143.6 1.3 broadcast_and_fusion.2
  145.2 25.4 %fusion.217 = (f32[2,512]{1,0:T(2,128)S(1)}, f32[2,512,5120]{2,1,0:T(8,128)}) fusion(f32[2,512,5120]{2,1,0:T(8,128)} %fusion.215, pred[512,5120]{1,0:T(8,128)(4,1)S(1)} %pad_add_fusion.2), kind=kOutput, calls=%fused_computation.273.clone.1 | output fusion | flops 36705280 | bytes 44568576 | tf_op jit(solution)/shard_map/while/body/eval_jaxpr/sub | solution.py:135
  170.6 8.8 %fusion.218 = bf16[2,512,2,80]{1,3,2,0:T(8,128)(2,1)S(1)} fusion(bf16[2,512,2,80]{1,3,2,0:T(8,128)(2,1)S(1)} %copy-done.6, s32[]{:T(128)S(6)} %copy.93, bf16[5120,2,80]{0,2,1:T(8,128)(2,1)S(1)} %copy-done.3, f32[2,512,5120]{2,1,0:T(8,128)} %get-tuple-element.254, f32[2,512]{1,0:T(2,128)S(1)} %get-tuple-element.255), kind=kOutput, calls=%fused_computation.15.clone.1 | convolution fusion | flops 849428480 | bytes 22777860 | tf_op jit(solution)/shard_map/while/body/eval_jaxpr/hqk,khd->qhd/dot_general | solution.py:137
  179.4 0.7 copy-done.7
  180.1 1.3 copy.57
  181.5 5.0 convolution_convert_fusion.1
  187.4 76.8 %reduce-scatter.3.cloned.1.call-done = bf16[64,2560]{1,0:T(8,128)(2,1)} async-done(((bf16[1024,2560]{1,0:T(8,128)(2,1)}), bf16[64,2560]{1,0:T(8,128)(2,1)}) %reduce-scatter.3.cloned.1.call-update) | async-done | bytes 327696 | tf_op jit(solution)/shard_map/reduce_scatter | solution.py:143
  264.2 1.3 fusion.63
  265.5 1.3 multiply_reduce_fusion.1
  266.9 2.0 add_convert_fusion.1
  269.2 2.4 convolution_convert_fusion.7
  271.9 0.7 copy.59
  272.6 2.2 fusion.23
  275.0 0.7 copy.61
  275.7 0.7 copy.60
  276.5 2.5 fusion.21
  279.1 14.9 %all-gather = f32[128,2,80]{2,1,0:T(2,128)S(1)} all-gather(f32[16,2,80]{2,1,0:T(2,128)S(1)} %multiply_add_fusion), channel_id=2, replica_groups=mesh['rep'=8,'tensor'=16] {'rep'}, dimensions={0}, use_global_device_ids=true | all-gather | bytes 92160 | tf_op jit(solution)/shard_map/all_gather | solution.py:10
  294.0 0.7 slice.109
  294.6 0.8 fusion.70
  295.5 0.7 fusion.116
  296.2 10.2 %all_gather.26 = f32[8,16,2]{1,2,0:T(2,128)S(1)} all-gather(f32[1,16,2]{1,2,0:T(2,128)S(1)} %get-tuple-element.148), channel_id=1, replica_groups=mesh['rep'=8,'tensor'=16] {'rep'}, dimensions={0}, use_global_device_ids=true | all-gather | bytes 1152 | tf_op jit(solution)/shard_map/all_gather | solution.py:10
  306.4 8.1 %all_gather.27 = f32[8,16,2]{1,2,0:T(2,128)S(1)} all-gather(f32[1,16,2]{1,2,0:T(2,128)S(1)} %get-tuple-element.147), channel_id=1, replica_groups=mesh['rep'=8,'tensor'=16] {'rep'}, dimensions={0}, use_global_device_ids=true | all-gather | bytes 1152 | tf_op jit(solution)/shard_map/all_gather | solution.py:10
  314.5 7.4 %while.25 = (s32[]{:T(128)}, f32[16,2]{0,1:T(2,128)S(1)}, f32[16,2]{0,1:T(2,128)S(1)}, f32[16,2,80]{2,1,0:T(2,128)S(1)}, f32[7,16,2]{1,2,0:T(2,128)S(1)}, /*inde...) while((s32[]{:T(128)}, f32[16,2]{0,1:T(2,128)S(1)}, f32[16,2]{0,1:T(2,128)S(1)}, ...), condition=%wide.region_14.15_spmd, body=%wide.region_13.14_spmd.sunk | while | flops 7874 | bytes 32613 | solution.py:13
  314.7 0.9 fusion.220
  315.7 0.9 fusion.220
  316.8 0.9 fusion.220
  317.9 0.9 fusion.220
  318.9 0.9 fusion.220
  320.0 0.9 fusion.220
  321.1 0.9 fusion.220
  322.2 2.0 convolution_convert_fusion.3
  324.3 1.5 all-gather.7.cloned.1.call-done
  325.7 17.9 %convolution_convert_fusion = bf16[1024,2560]{1,0:T(8,128)(2,1)} fusion(bf16[640,2560]{1,0:T(8,128)(2,1)S(1)} %copy-done, bf16[1024,2560]{1,0:T(8,128)(2,1)} %all-gather.7.cloned.1.call-done, bf16[2560,640]{1,0:T(8,128)(2,1)} %param.29, f32[640]{0:T(1024)} %param.30), kind=kOutput, calls=%fused_computation.33 | convolution fusion | flops 6756761600 | bytes 17041920 | tf_op jit(solution)/shard_map/dot_general | solution.py:160
  343.8 64.3 %all-reduce.3.cloned.1.call-done = bf16[16,2560]{1,0:T(8,128)(2,1)} async-done(((bf16[16,2560]{1,0:T(8,128)(2,1)}), bf16[16,2560]{1,0:T(8,128)(2,1)}) %all-reduce.3.cloned.1.call-update) | async-done | bytes 81936 | tf_op jit(solution)/shard_map/psum | solution.py:149
  408.1 1.0 fusion.65
  409.1 1.1 multiply_reduce_fusion.3
  410.2 1.0 add_convert_fusion.3
  411.2 3.6 convolution_convert_fusion.2
  414.9 75.9 %reduce-scatter.5.cloned.1.call-done = bf16[64,2560]{1,0:T(8,128)(2,1)} async-done(((bf16[1024,2560]{1,0:T(8,128)(2,1)}), bf16[64,2560]{1,0:T(8,128)(2,1)}) %reduce-scatter.5.cloned.1.call-update) | async-done | bytes 327696 | tf_op jit(solution)/shard_map/reduce_scatter | solution.py:159
  490.8 1.3 fusion.64
  492.1 1.3 multiply_reduce_fusion
  493.4 2.0 add_convert_fusion
  495.4 78.8 %all-reduce.5.cloned.1.call-done = bf16[16,2560]{1,0:T(8,128)(2,1)} async-done(((bf16[16,2560]{1,0:T(8,128)(2,1)}), bf16[16,2560]{1,0:T(8,128)(2,1)}) %all-reduce.5.cloned.1.call-update) | async-done | bytes 81936 | tf_op jit(solution)/shard_map/psum | solution.py:169
  574.3 1.0 fusion.66
  575.3 1.1 multiply_reduce_fusion.2
  576.4 1.0 add_convert_fusion.2
  577.4 3.1 convolution_convert_fusion.6
  580.5 54.0 %all-gather.9.cloned.1.call-done = bf16[1024,2560]{1,0:T(8,128)(2,1)} async-done(((bf16[64,2560]{1,0:T(8,128)(2,1)}), bf16[1024,2560]{1,0:T(8,128)(2,1)}) %all-gather.9.cloned.1.call-update) | async-done | bytes 5242896 | tf_op jit(solution)/shard_map/all_gather | solution.py:176
  634.5 6.9 %convolution_convert_fusion.4 = bf16[1024,480]{0,1:T(8,128)(2,1)} fusion(bf16[1024,2560]{1,0:T(8,128)(2,1)} %all-gather.9.cloned.1.call-done, bf16[2560,480]{0,1:T(8,128)(2,1)} %param.35), kind=kOutput, calls=%fused_computation.62 | convolution fusion | flops 2517073920 | bytes 8683520 | tf_op jit(solution)/shard_map/dot_general | solution.py:85
  (116 shorter events, 7.3 us)
Async XLA Ops:
  7.2 318.6 %copy-start = (bf16[640,2560]{1,0:T(8,128)(2,1)S(1)}, bf16[640,2560]{1,0:T(8,128)(2,1)}, u32[]{:S(2)}) copy-start(bf16[640,2560]{1,0:T(8,128)(2,1)} %param.31) | copy-start | bytes 9830404
  7.2 62.5 %all-gather.5.cloned.1.call-start = ((), (), s32[]{:S(2)}) async-start(), calls=%async_computation.2 | async-start | bytes 5570560 | tf_op jit(solution)/shard_map/all_gather | solution.py:88
  7.9 256.3 %reduce-scatter.3.cloned.1.call-start = ((), (), s32[]{:S(2)}) async-start(), calls=%async_computation.3 | async-start | bytes 5570560 | tf_op jit(solution)/shard_map/reduce_scatter | solution.py:143
  69.7 6.9 %copy-start.2 = (bf16[4096,2,80]{0,2,1:T(8,128)(2,1)S(1)}, bf16[4096,2,80]{0,2,1:T(8,128)(2,1)}, u32[]{:S(2)}) copy-start(bf16[4096,2,80]{0,2,1:T(8,128)(2,1)} %get-tuple-element.139) | copy-start | bytes 3932164
  75.7 1.4 copy-start.1
  77.2 2.0 copy-start.8
  94.7 25.4 %copy-start.3 = (bf16[5120,2,80]{0,2,1:T(8,128)(2,1)S(1)}, bf16[5120,2,80]{0,2,1:T(8,128)(2,1)}, u32[]{:S(2)}) copy-start(bf16[5120,2,80]{0,2,1:T(8,128)(2,1)} %get-tuple-element.301) | copy-start | bytes 4915204 | tf_op jit(solution)/shard_map/while
  94.7 25.4 %copy-start.6 = (bf16[2,512,2,80]{1,3,2,0:T(8,128)(2,1)S(1)}, bf16[2,512,2,80]{1,3,2,0:T(8,128)(2,1)}, u32[]{:S(2)}) copy-start(bf16[2,512,2,80]{1,3,2,0:T(8,128)(2,1)} %get-tuple-element.281) | copy-start | bytes 983044 | tf_op jit(solution)/shard_map/while
  128.9 0.7 copy-start.7
  145.1 25.4 %copy-start.3 = (bf16[5120,2,80]{0,2,1:T(8,128)(2,1)S(1)}, bf16[5120,2,80]{0,2,1:T(8,128)(2,1)}, u32[]{:S(2)}) copy-start(bf16[5120,2,80]{0,2,1:T(8,128)(2,1)} %get-tuple-element.301) | copy-start | bytes 4915204 | tf_op jit(solution)/shard_map/while
  145.2 25.4 %copy-start.6 = (bf16[2,512,2,80]{1,3,2,0:T(8,128)(2,1)S(1)}, bf16[2,512,2,80]{1,3,2,0:T(8,128)(2,1)}, u32[]{:S(2)}) copy-start(bf16[2,512,2,80]{1,3,2,0:T(8,128)(2,1)} %get-tuple-element.281) | copy-start | bytes 983044 | tf_op jit(solution)/shard_map/while
  179.4 0.7 copy-start.7
  186.5 0.7 copy-start.12
  186.5 0.8 copy-start.13
  186.5 0.8 copy-start.14
  186.6 82.6 %copy-start.4 = (bf16[16,2560]{1,0:T(8,128)(2,1)S(1)}, bf16[16,2560]{1,0:T(8,128)(2,1)}, u32[]{:S(2)}) copy-start(bf16[16,2560]{1,0:T(8,128)(2,1)} %param.21) | copy-start | bytes 245764
  186.6 139.2 %all-gather.7.cloned.1.call-start = ((), (), s32[]{:S(2)}) async-start(), calls=%async_computation.4 | async-start | bytes 5570560 | tf_op jit(solution)/shard_map/all_gather | solution.py:155
  264.2 8.4 %copy-start.17 = (s32[16]{0:T(128)S(1)}, s32[16]{0:T(128)}, u32[]{:S(2)}) copy-start(s32[16]{0:T(128)} %param.24) | copy-start | bytes 196
  268.9 139.2 %all-reduce.3.cloned.1.call-start = ((), (), s32[]{:S(2)}) async-start(), calls=%async_computation.7 | async-start | bytes 163840 | tf_op jit(solution)/shard_map/psum | solution.py:149
  272.6 2.4 copy-start.15
  274.9 4.0 copy-start.11
  276.3 2.6 copy-start.9
  276.3 2.7 copy-start.10
  324.2 166.5 %reduce-scatter.5.cloned.1.call-start = ((), (), s32[]{:S(2)}) async-start(), calls=%async_computation.5 | async-start | bytes 5570560 | tf_op jit(solution)/shard_map/reduce_scatter | solution.py:159
  343.7 67.5 %copy-start.16 = (f32[640]{0:T(1024)S(1)}, f32[640]{0:T(1024)}, u32[]{:S(2)}) copy-start(f32[640]{0:T(1024)} %param.30) | copy-start | bytes 7684
  343.7 230.6 %all-reduce.5.cloned.1.call-start = ((), (), s32[]{:S(2)}) async-start(), calls=%async_computation.8 | async-start | bytes 163840 | tf_op jit(solution)/shard_map/psum | solution.py:169
  414.9 219.7 %all-gather.9.cloned.1.call-start = ((), (), s32[]{:S(2)}) async-start(), calls=%async_computation.6 | async-start | bytes 5570560 | tf_op jit(solution)/shard_map/all_gather | solution.py:176
  577.4 64.1 %copy-start.5 = (bf16[16,2560]{1,0:T(8,128)(2,1)}, bf16[16,2560]{1,0:T(8,128)(2,1)S(1)}, u32[]{:S(2)}) copy-start(bf16[16,2560]{1,0:T(8,128)(2,1)S(1)} %add_convert_fusion.2) | copy-start | bytes 245764
Sparse Core Ops, SparseCore 0:
  10.2 59.4 all-gather.4
  186.7 77.4 reduce-scatter.2
  269.0 56.6 all-gather.6
  329.4 78.6 all-reduce.2
  411.7 79.0 reduce-scatter.4
  494.8 79.4 all-reduce.4
  577.0 57.4 all-gather.8
where the time goes:
time: 650 us; the launch traced here: 648 us
  waiting for transfers between devices  410 us (63%)
  matrix products  92.4 us (14%)
  other arithmetic  82.2 us (13%)
  blocking collectives  33.2 us (5%)
  between operations  14.4 us (2%)
  local copies, waits for them, and re-layouts  14.1 us (2%)
    psum x1, waiting for transfers between devices, per_device(): lax.psum(jnp.dot(dec_hidden, w_down, preferred_element_type=jnp.float32)....  78.8 us
    reduce_scatter x1, waiting for transfers between devices, per_device(): lax.psum_scatter(jnp.dot(attn, w_out, preferred_element_type=jnp.float32)...  76.8 us
    reduce_scatter x1, waiting for transfers between devices, per_device(): lax.psum_scatter(jnp.dot(hidden, w_down, preferred_element_type=jnp.float...  75.9 us
    psum x1, waiting for transfers between devices, per_device(): lax.psum(jnp.dot(dec_attn, w_out, preferred_element_type=jnp.float32).ast...  64.3 us
    all_gather x1, waiting for transfers between devices, per_device(): lax.all_gather(x_pre, 'tensor', axis=0, tiled=True)  58 us
    all_gather x1, waiting for transfers between devices, per_device(): lax.all_gather(layer_out, 'tensor', axis=0, tiled=True)  54 us
    sub x2, other arithmetic, attend_block(): weights = jnp.where(mask[None], jnp.exp(scores - highest), 0.0)  50.8 us
    all_gather x3, blocking collectives, combined_all(): pieces = jax.tree.map(lambda part: lax.all_gather(part, axis), value)  33.2 us
  transfers between devices with their start and end apart: 7, of which 7 were waited for; matrix products, arithmetic and copies ran while one was open for 9% of the time, Pallas kernels for 0%

commit v1 on v0

--- a/solution.py
+++ b/solution.py
@@ -173,7 +173,11 @@
     dec_out = layer_norm(
         dec_first.astype(jnp.float32) + dec_mlp + biases[1], gains[1], shifts[1]
     ).astype(jnp.bfloat16)
-    next_qkv = next_rows(lax.all_gather(layer_out, "tensor", axis=0, tiled=True))
+    next_qkv = next_rows(
+        jnp.concatenate(
+            lax.all_to_all(jnp.stack([layer_out] * lax.axis_size("tensor")), "tensor", 0, 0), axis=0
+        )
+    )
     dec_next_qkv = next_rows(dec_out)
     return (layer_out, next_qkv, dec_out, dec_next_qkv)
 

time: 650 us -> 670 us (1.031)
  waiting for transfers between devices: 410 us -> 421 us
    all_gather x1, waiting for transfers between devices: 1.47 us -> 56.8 us  [per_device(): hidden = up_rows(lax.all_gather(h_first, 'tensor', axis=0, tiled=True))]
    all_gather x1 -> x0, waiting for transfers between devices: 54 us -> none  [per_device(): lax.all_gather(layer_out, 'tensor', axis=0, tiled=True)]
    psum x1, waiting for transfers between devices: 64.3 us -> 116 us  [per_device(): lax.psum(jnp.dot(dec_attn, w_out, preferred_element_type=jnp.float32).ast...]
    reduce_scatter x1, waiting for transfers between devices: 75.9 us -> 32.7 us  [per_device(): lax.psum_scatter(jnp.dot(hidden, w_down, preferred_element_type=jnp.float...]
  transfers between devices with their start and end apart: 7 -> 7, of which waited for: 7 -> 6; matrix products, arithmetic and copies ran while one was open for 9% -> 6% of each run, Pallas kernels for 0% -> 0%
where the time goes in v1:
time: 670 us; the launch traced here: 667 us
  waiting for transfers between devices  421 us (63%)
  matrix products  92.5 us (14%)
  other arithmetic  81.5 us (12%)
  blocking collectives  32.1 us (5%)
  local copies, waits for them, and re-layouts  18.5 us (3%)
  between operations  14.4 us (2%)
    psum x1, waiting for transfers between devices, per_device(): lax.psum(jnp.dot(dec_attn, w_out, preferred_element_type=jnp.float32).ast...  116 us
    psum x1, waiting for transfers between devices, per_device(): lax.psum(jnp.dot(dec_hidden, w_down, preferred_element_type=jnp.float32)....  80.4 us
    reduce_scatter x1, waiting for transfers between devices, per_device(): lax.psum_scatter(jnp.dot(attn, w_out, preferred_element_type=jnp.float32)...  76.8 us
    all_gather x1, waiting for transfers between devices, per_device(): lax.all_gather(x_pre, 'tensor', axis=0, tiled=True)  58 us
    all_gather x1, waiting for transfers between devices, per_device(): hidden = up_rows(lax.all_gather(h_first, 'tensor', axis=0, tiled=True))  56.8 us
    sub x2, other arithmetic, attend_block(): weights = jnp.where(mask[None], jnp.exp(scores - highest), 0.0)  50.8 us
    reduce_scatter x1, waiting for transfers between devices, per_device(): lax.psum_scatter(jnp.dot(hidden, w_down, preferred_element_type=jnp.float...  32.7 us
    all_gather x3, blocking collectives, combined_all(): pieces = jax.tree.map(lambda part: lax.all_gather(part, axis), value)  32.1 us
  transfers between devices with their start and end apart: 7, of which 6 were waited for; matrix products, arithmetic and copies ran while one was open for 6% of the time, Pallas kernels for 0%

profile of v1, /device:TPU:1, one launch (start us, length us, event | category | flops | bytes accessed | tf_op | source)
XLA Modules:
  0.0 667.3 jit_solution(16160523475279774402)
XLA Ops:
  7.2 0.7 all-gather.4.cloned.1.call-update
  8.0 3.7 fusion.182
  11.7 58.0 %all-gather.4.cloned.1.call-done = bf16[1024,2560]{1,0:T(8,128)(2,1)} async-done(((bf16[64,2560]{1,0:T(8,128)(2,1)}), bf16[1024,2560]{1,0:T(8,128)(2,1)}) %all-gather.4.cloned.1.call-update) | async-done | bytes 5242896 | tf_op jit(solution)/shard_map/all_gather | solution.py:88
  69.7 6.1 convolution_convert_fusion.5
  75.8 0.8 slice_bitcast_fusion
  77.2 2.0 pad_maximum_fusion
  79.2 101.0 %while.24 = (s32[]{:T(128)}, bf16[2,512,2,80]{1,3,2,0:T(8,128)(2,1)}, s32[]{:T(128)}, s32[2]{0:T(128)S(1)}, s32[1024]{0:T(1024)S(1)}, /*index=5*/s32[1,1024]{1,0...) while((s32[]{:T(128)}, ...), condition=%wide.region_3.4_spmd, body=%wide.region_0.3_spmd.sunk | while | flops 1731291136 | bytes 107183400 | solution.py:141
  80.4 11.4 %fusion.215 = f32[2,512,5120]{2,1,0:T(8,128)} fusion(bf16[5120,2,80]{0,2,1:T(8,128)(2,1)} %get-tuple-element.300, bf16[1024,2,80]{0,2,1:T(8,128)(2,1)} %get-tuple-element.299, s32[]{:T(128)S(6)} %select_n.124), kind=kOutput, calls=%fused_computation.16.clone.1 | convolution fusion | flops 838860800 | bytes 22773764 | tf_op jit(solution)/shard_map/while/body/eval_jaxpr/qhd,khd->hqk/dot_general | solution.py:131
  93.2 1.3 broadcast_and_fusion.2
  94.7 25.4 %fusion.217 = (f32[2,512]{1,0:T(2,128)S(1)}, f32[2,512,5120]{2,1,0:T(8,128)}) fusion(f32[2,512,5120]{2,1,0:T(8,128)} %fusion.215, pred[512,5120]{1,0:T(8,128)(4,1)S(1)} %pad_add_fusion.2), kind=kOutput, calls=%fused_computation.273.clone.1 | output fusion | flops 36705280 | bytes 44568576 | tf_op jit(solution)/shard_map/while/body/eval_jaxpr/sub | solution.py:135
  120.1 8.8 %fusion.218 = bf16[2,512,2,80]{1,3,2,0:T(8,128)(2,1)S(1)} fusion(bf16[2,512,2,80]{1,3,2,0:T(8,128)(2,1)S(1)} %copy-done.7, s32[]{:T(128)S(6)} %copy.93, bf16[5120,2,80]{0,2,1:T(8,128)(2,1)S(1)} %copy-done.3, f32[2,512,5120]{2,1,0:T(8,128)} %get-tuple-element.254, f32[2,512]{1,0:T(2,128)S(1)} %get-tuple-element.255), kind=kOutput, calls=%fused_computation.15.clone.1 | convolution fusion | flops 849428480 | bytes 22777860 | tf_op jit(solution)/shard_map/while/body/eval_jaxpr/hqk,khd->qhd/dot_general | solution.py:137
  128.9 0.7 copy-done.8
  130.9 11.4 %fusion.215 = f32[2,512,5120]{2,1,0:T(8,128)} fusion(bf16[5120,2,80]{0,2,1:T(8,128)(2,1)} %get-tuple-element.300, bf16[1024,2,80]{0,2,1:T(8,128)(2,1)} %get-tuple-element.299, s32[]{:T(128)S(6)} %select_n.124), kind=kOutput, calls=%fused_computation.16.clone.1 | convolution fusion | flops 838860800 | bytes 22773764 | tf_op jit(solution)/shard_map/while/body/eval_jaxpr/qhd,khd->hqk/dot_general | solution.py:131
  143.6 1.3 broadcast_and_fusion.2
  145.2 25.4 %fusion.217 = (f32[2,512]{1,0:T(2,128)S(1)}, f32[2,512,5120]{2,1,0:T(8,128)}) fusion(f32[2,512,5120]{2,1,0:T(8,128)} %fusion.215, pred[512,5120]{1,0:T(8,128)(4,1)S(1)} %pad_add_fusion.2), kind=kOutput, calls=%fused_computation.273.clone.1 | output fusion | flops 36705280 | bytes 44568576 | tf_op jit(solution)/shard_map/while/body/eval_jaxpr/sub | solution.py:135
  170.6 8.8 %fusion.218 = bf16[2,512,2,80]{1,3,2,0:T(8,128)(2,1)S(1)} fusion(bf16[2,512,2,80]{1,3,2,0:T(8,128)(2,1)S(1)} %copy-done.7, s32[]{:T(128)S(6)} %copy.93, bf16[5120,2,80]{0,2,1:T(8,128)(2,1)S(1)} %copy-done.3, f32[2,512,5120]{2,1,0:T(8,128)} %get-tuple-element.254, f32[2,512]{1,0:T(2,128)S(1)} %get-tuple-element.255), kind=kOutput, calls=%fused_computation.15.clone.1 | convolution fusion | flops 849428480 | bytes 22777860 | tf_op jit(solution)/shard_map/while/body/eval_jaxpr/hqk,khd->qhd/dot_general | solution.py:137
  179.4 0.7 copy-done.8
  180.1 1.3 copy.57
  181.5 5.0 convolution_convert_fusion.1
  187.4 76.8 %reduce-scatter.3.cloned.1.call-done = bf16[64,2560]{1,0:T(8,128)(2,1)} async-done(((bf16[1024,2560]{1,0:T(8,128)(2,1)}), bf16[64,2560]{1,0:T(8,128)(2,1)}) %reduce-scatter.3.cloned.1.call-update) | async-done | bytes 327696 | tf_op jit(solution)/shard_map/reduce_scatter | solution.py:143
  264.2 1.3 fusion.63
  265.5 1.3 multiply_reduce_fusion.1
  266.9 2.0 add_convert_fusion.1
  268.9 56.8 %all-gather.6.cloned.1.call-done = bf16[1024,2560]{1,0:T(8,128)(2,1)} async-done(((bf16[64,2560]{1,0:T(8,128)(2,1)}), bf16[1024,2560]{1,0:T(8,128)(2,1)}) %all-gather.6.cloned.1.call-update) | async-done | bytes 5242896 | tf_op jit(solution)/shard_map/all_gather | solution.py:155
  325.7 17.9 %convolution_convert_fusion = bf16[1024,2560]{1,0:T(8,128)(2,1)} fusion(bf16[640,2560]{1,0:T(8,128)(2,1)S(1)} %copy-done, bf16[1024,2560]{1,0:T(8,128)(2,1)} %all-gather.6.cloned.1.call-done, bf16[2560,640]{1,0:T(8,128)(2,1)} %param.29, f32[640]{0:T(1024)S(1)} %copy-done.17), kind=kOutput, calls=%fused_computation.33 | convolution fusion | flops 6756761600 | bytes 17041920 | tf_op jit(solution)/shard_map/dot_general | solution.py:160
  343.7 0.8 copy-done.4
  344.5 2.4 convolution_convert_fusion.7
  347.2 0.7 copy.59
  348.0 2.2 fusion.23
  350.3 0.7 copy.61
  351.0 0.7 copy.60
  351.8 2.7 fusion.21
  354.6 13.7 %all-gather = f32[128,2,80]{2,1,0:T(2,128)S(1)} all-gather(f32[16,2,80]{2,1,0:T(2,128)S(1)} %multiply_add_fusion), channel_id=2, replica_groups=mesh['rep'=8,'tensor'=16] {'rep'}, dimensions={0}, use_global_device_ids=true | all-gather | bytes 92160 | tf_op jit(solution)/shard_map/all_gather | solution.py:10
  369.0 0.8 fusion.70
  369.9 0.7 fusion.116
  370.6 10.2 %all_gather.22 = f32[8,16,2]{1,2,0:T(2,128)S(1)} all-gather(f32[1,16,2]{1,2,0:T(2,128)S(1)} %get-tuple-element.148), channel_id=1, replica_groups=mesh['rep'=8,'tensor'=16] {'rep'}, dimensions={0}, use_global_device_ids=true | all-gather | bytes 1152 | tf_op jit(solution)/shard_map/all_gather | solution.py:10
  380.8 8.1 %all_gather.23 = f32[8,16,2]{1,2,0:T(2,128)S(1)} all-gather(f32[1,16,2]{1,2,0:T(2,128)S(1)} %get-tuple-element.147), channel_id=1, replica_groups=mesh['rep'=8,'tensor'=16] {'rep'}, dimensions={0}, use_global_device_ids=true | all-gather | bytes 1152 | tf_op jit(solution)/shard_map/all_gather | solution.py:10
  388.9 32.7 %reduce-scatter.5.cloned.1.call-done = bf16[64,2560]{1,0:T(8,128)(2,1)} async-done(((bf16[1024,2560]{1,0:T(8,128)(2,1)}), bf16[64,2560]{1,0:T(8,128)(2,1)}) %reduce-scatter.5.cloned.1.call-update) | async-done | bytes 327696 | tf_op jit(solution)/shard_map/reduce_scatter | solution.py:159
  421.6 1.3 fusion.64
  422.9 1.3 multiply_reduce_fusion
  424.2 1.3 add_convert_fusion
  425.6 0.7 copy-done.5
  426.3 2.9 stack.2
  429.1 4.8 all-to-all-start
  434.0 7.4 %while.25 = (s32[]{:T(128)}, f32[16,2]{0,1:T(2,128)S(1)}, f32[16,2]{0,1:T(2,128)S(1)}, f32[16,2,80]{2,1,0:T(2,128)S(1)}, f32[7,16,2]{1,2,0:T(2,128)S(1)}, /*inde...) while((s32[]{:T(128)}, f32[16,2]{0,1:T(2,128)S(1)}, f32[16,2]{0,1:T(2,128)S(1)}, ...), condition=%wide.region_14.15_spmd, body=%wide.region_13.14_spmd.sunk | while | flops 7874 | bytes 32613 | solution.py:13
  434.2 0.9 fusion.220
  435.2 0.9 fusion.220
  436.3 0.9 fusion.220
  437.4 0.9 fusion.220
  438.4 0.9 fusion.220
  439.5 0.9 fusion.220
  440.6 0.9 fusion.220
  441.7 2.0 convolution_convert_fusion.3
  444.0 116.1 %all-reduce.3.cloned.1.call-done = bf16[16,2560]{1,0:T(8,128)(2,1)} async-done(((bf16[16,2560]{1,0:T(8,128)(2,1)}), bf16[16,2560]{1,0:T(8,128)(2,1)}) %all-reduce.3.cloned.1.call-update) | async-done | bytes 81936 | tf_op jit(solution)/shard_map/psum | solution.py:149
  560.1 1.0 fusion.65
  561.1 1.1 multiply_reduce_fusion.3
  562.2 1.0 add_convert_fusion.3
  563.2 3.6 convolution_convert_fusion.2
  566.8 80.4 %all-reduce.5.cloned.1.call-done = bf16[16,2560]{1,0:T(8,128)(2,1)} async-done(((bf16[16,2560]{1,0:T(8,128)(2,1)}), bf16[16,2560]{1,0:T(8,128)(2,1)}) %all-reduce.5.cloned.1.call-update) | async-done | bytes 81936 | tf_op jit(solution)/shard_map/psum | solution.py:169
  647.2 1.0 fusion.66
  648.3 1.1 multiply_reduce_fusion.2
  649.4 1.0 add_convert_fusion.2
  650.4 3.1 convolution_convert_fusion.6
  653.5 6.9 %convolution_convert_fusion.4 = bf16[1024,480]{0,1:T(8,128)(2,1)} fusion(bf16[1024,2560]{1,0:T(8,128)(2,1)} %bitcast.14, bf16[2560,480]{0,1:T(8,128)(2,1)} %param.35), kind=kOutput, calls=%fused_computation.62 | convolution fusion | flops 2517073920 | bytes 8683520 | tf_op jit(solution)/shard_map/dot_general | solution.py:85
  (120 shorter events, 9.3 us)
Async XLA Ops:
  7.2 318.6 %copy-start = (bf16[640,2560]{1,0:T(8,128)(2,1)S(1)}, bf16[640,2560]{1,0:T(8,128)(2,1)}, u32[]{:S(2)}) copy-start(bf16[640,2560]{1,0:T(8,128)(2,1)} %param.31) | copy-start | bytes 9830404
  7.2 62.5 %all-gather.4.cloned.1.call-start = ((), (), s32[]{:S(2)}) async-start(), calls=%async_computation.3 | async-start | bytes 5570560 | tf_op jit(solution)/shard_map/all_gather | solution.py:88
  7.9 256.3 %reduce-scatter.3.cloned.1.call-start = ((), (), s32[]{:S(2)}) async-start(), calls=%async_computation.4 | async-start | bytes 5570560 | tf_op jit(solution)/shard_map/reduce_scatter | solution.py:143
  69.7 6.9 %copy-start.2 = (bf16[4096,2,80]{0,2,1:T(8,128)(2,1)S(1)}, bf16[4096,2,80]{0,2,1:T(8,128)(2,1)}, u32[]{:S(2)}) copy-start(bf16[4096,2,80]{0,2,1:T(8,128)(2,1)} %get-tuple-element.139) | copy-start | bytes 3932164
  75.7 1.4 copy-start.1
  77.2 2.0 copy-start.9
  94.7 25.4 %copy-start.3 = (bf16[5120,2,80]{0,2,1:T(8,128)(2,1)S(1)}, bf16[5120,2,80]{0,2,1:T(8,128)(2,1)}, u32[]{:S(2)}) copy-start(bf16[5120,2,80]{0,2,1:T(8,128)(2,1)} %get-tuple-element.301) | copy-start | bytes 4915204 | tf_op jit(solution)/shard_map/while
  94.7 25.4 %copy-start.7 = (bf16[2,512,2,80]{1,3,2,0:T(8,128)(2,1)S(1)}, bf16[2,512,2,80]{1,3,2,0:T(8,128)(2,1)}, u32[]{:S(2)}) copy-start(bf16[2,512,2,80]{1,3,2,0:T(8,128)(2,1)} %get-tuple-element.281) | copy-start | bytes 983044 | tf_op jit(solution)/shard_map/while
  128.9 0.7 copy-start.8
  145.1 25.4 %copy-start.3 = (bf16[5120,2,80]{0,2,1:T(8,128)(2,1)S(1)}, bf16[5120,2,80]{0,2,1:T(8,128)(2,1)}, u32[]{:S(2)}) copy-start(bf16[5120,2,80]{0,2,1:T(8,128)(2,1)} %get-tuple-element.301) | copy-start | bytes 4915204 | tf_op jit(solution)/shard_map/while
  145.2 25.4 %copy-start.7 = (bf16[2,512,2,80]{1,3,2,0:T(8,128)(2,1)S(1)}, bf16[2,512,2,80]{1,3,2,0:T(8,128)(2,1)}, u32[]{:S(2)}) copy-start(bf16[2,512,2,80]{1,3,2,0:T(8,128)(2,1)} %get-tuple-element.281) | copy-start | bytes 983044 | tf_op jit(solution)/shard_map/while
  179.4 0.7 copy-start.8
  186.5 0.7 copy-start.13
  186.5 0.8 copy-start.14
  186.5 0.8 copy-start.15
  186.6 139.2 %copy-start.17 = (f32[640]{0:T(1024)S(1)}, f32[640]{0:T(1024)}, u32[]{:S(2)}) copy-start(f32[640]{0:T(1024)} %param.30) | copy-start | bytes 7684
  186.6 139.1 %all-gather.6.cloned.1.call-start = ((), (), s32[]{:S(2)}) async-start(), calls=%async_computation.5 | async-start | bytes 5570560 | tf_op jit(solution)/shard_map/all_gather | solution.py:155
  268.9 152.7 %reduce-scatter.5.cloned.1.call-start = ((), (), s32[]{:S(2)}) async-start(), calls=%async_computation.6 | async-start | bytes 5570560 | tf_op jit(solution)/shard_map/reduce_scatter | solution.py:159
  343.6 0.9 copy-start.4
  343.7 4.3 copy-start.19
  347.9 2.4 copy-start.16
  350.3 4.2 copy-start.12
  351.7 2.9 copy-start.10
  351.7 2.9 copy-start.11
  425.5 0.7 copy-start.5
  429.1 134.1 %copy-start.18 = (f32[640]{0:T(1024)S(1)}, f32[640]{0:T(1024)}, u32[]{:S(2)}) copy-start(f32[640]{0:T(1024)} %param.30) | copy-start | bytes 7684
  429.1 224.4 %all-to-all-start = ((bf16[16,64,2560]{2,1,0:T(8,128)(2,1)}), bf16[16,64,2560]{2,1,0:T(8,128)(2,1)}, u32[]{:S(2)}, u32[]{:S(2)}) async-start(bf16[16,64,2560]{2,1,0:T(8,128)(2,1)} %stack.2), calls=%async_computation.2 | async-start | bytes 10485760 | tf_op jit(solution)/shard_map/all_to_all | solution.py:178
  433.9 126.2 %all-reduce.3.cloned.1.call-start = ((), (), s32[]{:S(2)}) async-start(), calls=%async_computation.7 | async-start | bytes 163840 | tf_op jit(solution)/shard_map/psum | solution.py:149
  443.7 203.5 %all-reduce.5.cloned.1.call-start = ((), (), s32[]{:S(2)}) async-start(), calls=%async_computation.8 | async-start | bytes 163840 | tf_op jit(solution)/shard_map/psum | solution.py:169
  650.4 10.1 %copy-start.6 = (bf16[16,2560]{1,0:T(8,128)(2,1)}, bf16[16,2560]{1,0:T(8,128)(2,1)S(1)}, u32[]{:S(2)}) copy-start(bf16[16,2560]{1,0:T(8,128)(2,1)S(1)} %add_convert_fusion.2) | copy-start | bytes 245764
Sparse Core Ops, SparseCore 0:
  10.2 59.4 all-gather.3
  186.7 77.4 reduce-scatter.2
  269.0 56.6 all-gather.5
  343.8 77.7 reduce-scatter.4
  443.8 116.2 all-reduce.2
  567.0 80.2 all-reduce.4
